TPU v7x, 512 devices: a whole 4x8x8 slice. The times are simulated.
512 devices in a mesh: pair: 16 (over x, y_lo), aux: 32 (over y_hi, z, core).
Axes of the slice: x: 4, y: 8 (y_hi: 2, y_lo: 4; y = y_hi * 4 + y_lo), z: 8, core: 2. Of those that a mesh axis runs over, the one named last changes fastest.
Arguments:
- amplitudes: bfloat16 [16, 512, 512], P('pair', 'aux'), may hold values from -6 to 6
- factors: bfloat16 [4096, 512, 512], P('aux', 'pair'), may hold values from -0.03125 to 0.03125
- hole_weights: float32 [16, 16], replicated, may hold values from -1.5 to 1.5
- driver: float32 [16, 6, 512], P('pair', None, 'aux'), may hold values from -6 to 6
- eps_vir: float32 [512], replicated, may hold values from 0.5 to 3
- pair_energy: float32 [16], P('pair'), may hold values from -3 to -0.5
Outputs:
- residual: float32 [16, 6, 512], P('pair', None, 'aux')
- new_amps: float32 [16, 6, 512], P('pair', None, 'aux')
All inputs are finite; a program needn't handle non-finite values.
Results may differ from a plain program's by a relative error of at most 0.0003.
Values may be sent and summed in bfloat16 or wider, within the bound.
No kernel may reach another device: no remote copies, remote signals or barrier semaphores. Data moves between devices by JAX's collectives and lax.ppermute only.
A program may use at most 64 MiB of HBM per device.

v0:
```python
import jax
import jax.numpy as jnp
from jax import lax
from jax.sharding import Mesh
from jax.sharding import PartitionSpec as P

PAIR = ("pair_0", "pair_1")


def sent_to_all(array, axis):
    count = lax.axis_size(axis)
    return lax.all_to_all(
        jnp.broadcast_to(array[None], (count, *array.shape)), axis, 0, 0, tiled=True
    )


def in_order(tiles, dim):
    tiles = jnp.moveaxis(tiles, 0, dim)
    shape = tiles.shape
    return tiles.reshape(*shape[:dim], shape[dim] * shape[dim + 1], *shape[dim + 2 :])


def collect(array, axis, dim):
    tiles = sent_to_all(array, axis)
    return in_order(tiles, dim)


def spread(array, axes, root):
    array = jnp.where(lax.axis_index(axes) == root, array, jnp.zeros_like(array))
    for axis in axes:
        array = lax.psum(array, axis)
    return array


def cut_along(array, dim, count):
    before, after = (array.shape[:dim], array.shape[dim + 1 :])
    return jnp.moveaxis(array.reshape(*before, count, -1, *after), dim, 0)


def sent_and_summed(array, axis, dim):
    count = lax.axis_size(axis)
    tiles = lax.all_to_all(cut_along(array, dim, count), axis, 0, 0, tiled=True)
    return jnp.sum(tiles, axis=0)


def half_of(window, amp_pair):
    return jnp.einsum("qac,cd->aqd", window, amp_pair, preferred_element_type=jnp.float32).astype(
        jnp.bfloat16
    )


def contract(halves, factors):
    return jnp.einsum("aqd,qbd->ab", halves, factors, preferred_element_type=jnp.float32)


def per_device(amplitudes, factors, hole_weights, driver, eps_vir, pair_energy):
    window_rows = driver.shape[1]
    columns = driver.shape[2]
    amp_full = collect(amplitudes, "aux", 1)
    window = spread(factors[:, :window_rows, :], PAIR, 0)
    amp_window = amp_full[:, :window_rows, :]
    slab = lax.all_to_all(amp_window, PAIR, split_axis=2, concat_axis=0, tiled=True)

    def ladder_pair(amp_pair):
        return contract(half_of(window, amp_pair), factors)

    particle = lax.map(ladder_pair, lax.all_gather(amp_full, PAIR, axis=0, tiled=True))
    hole_term = jnp.einsum(
        "pk,kab->pab", hole_weights, slab.astype(jnp.float32), precision=lax.Precision.HIGHEST
    )
    aux_index = lax.axis_index("aux")
    partial_value = particle + jnp.where(aux_index == 0, hole_term, 0.0)
    returned = lax.all_to_all(partial_value, PAIR, split_axis=0, concat_axis=2, tiled=True)
    summed = sent_and_summed(returned, "aux", 2)
    residual = driver + summed
    column_start = aux_index * columns
    amp_cols = lax.dynamic_slice_in_dim(amp_window, column_start, columns, 2).astype(jnp.float32)
    eps_cols = lax.dynamic_slice_in_dim(eps_vir, column_start, columns, 0)
    denominator = (
        eps_vir[:window_rows][None, :, None] + eps_cols[None, None, :] - pair_energy[:, None, None]
    )
    new_amps = amp_cols - residual / denominator
    return (residual, new_amps)


def solution(mesh):
    finer = Mesh(mesh.devices.reshape(4, 4, mesh.shape["aux"]), ("pair_0", "pair_1", "aux"))
    in_specs = (P(PAIR, "aux", None), P("aux", PAIR, None), P(), P(PAIR, None, "aux"), P(), P(PAIR))
    out_specs = (P(PAIR, None, "aux"), P(PAIR, None, "aux"))
    return jax.shard_map(
        per_device, mesh=finer, in_specs=in_specs, out_specs=out_specs, check_vma=False
    )
```

profile of v0, /device:TPU:1, one launch (start us, length us, event | category | flops | bytes accessed | tf_op | source)
XLA Modules:
  0.0 425.7 jit_solution(4023504486053572570)
XLA Ops:
  11.7 17.2 %all-to-all-start = ((bf16[32,1,16,512]{3,2,1,0:T(8,128)(2,1)}), bf16[32,1,16,512]{3,2,1,0:T(8,128)(2,1)S(1)}, u32[]{:S(2)}, u32[]{:S(2)}) async-start(bf16[32,1,16,512]{3,2,1,0:T(8,128)(2,1)} %broadcast_in_dim.25), calls=%async_computation | async-start | bytes 1048576 | tf_op jit(solution)/shard_map/all_to_all | solution.py:12
  29.0 41.0 %all-reduce.3.cloned.1.call-done = bf16[128,6,512]{2,0,1:T(8,128)(2,1)} async-done(((bf16[128,6,512]{2,0,1:T(8,128)(2,1)}), bf16[128,6,512]{2,0,1:T(8,128)(2,1)}) %all-reduce.3.cloned.1.call-update) | async-done | bytes 786448 | tf_op jit(solution)/shard_map/psum | solution.py:31
  72.5 6.1 %all-to-all-start.1 = ((bf16[1,6,512]{1,0,2:T(2,128)(2,1)}), bf16[1,6,512]{1,0,2:T(2,128)(2,1)S(1)}, u32[]{:S(2)}, u32[]{:S(2)}) async-start(bf16[1,6,512]{1,0,2:T(2,128)(2,1)} %copy.39), calls=%async_computation.1 | async-start | bytes 524288 | tf_op jit(solution)/shard_map/all_to_all | solution.py:62
  78.6 9.1 %copy.38 = bf16[128,32,512]{0,1,2:T(8,128)(2,1)} copy(bf16[128,32,512]{2,1,0:T(8,128)(2,1)} %param.9) | data formatting | bytes 8388608 | tf_op jit(solution)/shard_map/while | solution.py:67
  88.0 118.5 %all-reduce.5.cloned.1.call-done = bf16[128,6,512]{2,0,1:T(8,128)(2,1)} async-done(((bf16[128,6,512]{2,0,1:T(8,128)(2,1)}), bf16[128,6,512]{2,0,1:T(8,128)(2,1)}) %all-reduce.5.cloned.1.call-update) | async-done | bytes 786448 | tf_op jit(solution)/shard_map/psum | solution.py:31
  206.5 81.9 %all-gather.2.cloned.1.call-done = bf16[16,512,512]{2,1,0:T(8,128)(2,1)} async-done(((bf16[1,512,512]{2,1,0:T(8,128)(2,1)}), bf16[16,512,512]{2,1,0:T(8,128)(2,1)}) %all-gather.2.cloned.1.call-update) | async-done | bytes 8388624 | tf_op jit(solution)/shard_map/all_gather | solution.py:67
  288.4 88.9 %while.11 = (s32[]{:T(128)}, f32[16,6,32]{2,0,1:T(8,128)S(1)}, bf16[16,512,512]{2,1,0:T(8,128)(2,1)}, bf16[128,6,512]{2,0,1:T(8,128)(2,1)}, bf16[128,32,512]{0,1,2:T(8,128)(2,1)}) while((s32[]{:T(128)}, f32[16,6,32]{2,0,1:T(8,128)S(1)}, bf16[16,512,512]{2,1,0:T(8,128)(2,1)}, bf16[128,6,512]{2,0,1:T(8,128)(2,1)}, ...), condition=%wide.region_3.4_spmd.clone, body=%wide.region_2.3_spmd.sunk.clone | while | flops 428212224 | bytes 7081805 | solution.py:67
  290.3 3.6 convolution_bitcast_fusion.3
  295.9 3.6 convolution_bitcast_fusion.3
  301.5 3.6 convolution_bitcast_fusion.3
  307.0 3.6 convolution_bitcast_fusion.3
  312.6 3.6 convolution_bitcast_fusion.3
  318.1 3.6 convolution_bitcast_fusion.3
  323.7 3.6 convolution_bitcast_fusion.3
  329.2 3.6 convolution_bitcast_fusion.3
  334.8 3.6 convolution_bitcast_fusion.3
  340.4 3.6 convolution_bitcast_fusion.3
  345.9 3.6 convolution_bitcast_fusion.3
  351.5 3.6 convolution_bitcast_fusion.3
  362.6 3.6 convolution_bitcast_fusion.3
  368.2 3.6 convolution_bitcast_fusion.3
  377.6 10.4 %all_to_all.43 = f32[16,1,192]{2,1,0:T(1,128)S(1)} all-to-all(f32[16,1,192]{2,1,0:T(1,128)S(1)} %reshape.71), channel_id=1, replica_groups=mesh['pair_0'=4,'pair_1'=4,'aux'=32] {'pair_0','pair_1'}, dimensions={0} | all-to-all | bytes 24576 | tf_op jit(solution)/shard_map/all_to_all | solution.py:73
  390.1 14.9 %all-to-all-start.3 = ((f32[32,1,6,16]{3,1,2,0:T(1,128)}), f32[32,1,6,16]{3,1,2,0:T(1,128)S(1)}, u32[]{:S(2)}, u32[]{:S(2)}) async-start(f32[32,1,6,16]{3,1,2,0:T(1,128)} %copy.44), calls=%async_computation.3 | async-start | bytes 196608 | tf_op jit(solution)/shard_map/all_to_all | solution.py:42
  405.7 11.1 %all-to-all-done.3 = f32[32,1,6,16]{3,1,2,0:T(1,128)S(1)} async-done(((f32[32,1,6,16]{3,1,2,0:T(1,128)}), f32[32,1,6,16]{3,1,2,0:T(1,128)S(1)}, u32[]{:S(2)}, u32[]{:S(2)}) %all-to-all-start.3) | async-done | bytes 12320 | tf_op jit(solution)/shard_map/all_to_all | solution.py:42
  (92 shorter events, 48.9 us)
Async XLA Ops:
  8.0 369.3 %copy-start = (f32[16,16]{1,0:T(8,128)S(1)}, f32[16,16]{1,0:T(8,128)}, u32[]{:S(2)}) copy-start(f32[16,16]{1,0:T(8,128)} %param.10) | copy-start | bytes 3076
  8.0 2.8 copy-start.2
  8.0 62.0 %all-reduce.3.cloned.1.call-start = ((), (), s32[]{:S(2)}) async-start(), calls=%async_computation.5 | async-start | bytes 1572864 | tf_op jit(solution)/shard_map/psum | solution.py:31
  11.7 58.4 %all-to-all-start = ((bf16[32,1,16,512]{3,2,1,0:T(8,128)(2,1)}), bf16[32,1,16,512]{3,2,1,0:T(8,128)(2,1)S(1)}, u32[]{:S(2)}, u32[]{:S(2)}) async-start(bf16[32,1,16,512]{3,2,1,0:T(8,128)(2,1)} %broadcast_in_dim.25), calls=%async_computation | async-start | bytes 1048576 | tf_op jit(solution)/shard_map/all_to_all | solution.py:12
  29.0 177.6 %all-reduce.5.cloned.1.call-start = ((), (), s32[]{:S(2)}) async-start(), calls=%async_computation.6 | async-start | bytes 1572864 | tf_op jit(solution)/shard_map/psum | solution.py:31
  70.0 218.3 %all-gather.2.cloned.1.call-start = ((), (), s32[]{:S(2)}) async-start(), calls=%async_computation.4 | async-start | bytes 8912896 | tf_op jit(solution)/shard_map/all_gather | solution.py:67
  70.1 0.8 copy-start.1
  72.5 15.2 %all-to-all-start.1 = ((bf16[1,6,512]{1,0,2:T(2,128)(2,1)}), bf16[1,6,512]{1,0,2:T(2,128)(2,1)S(1)}, u32[]{:S(2)}, u32[]{:S(2)}) async-start(bf16[1,6,512]{1,0,2:T(2,128)(2,1)} %copy.39), calls=%async_computation.1 | async-start | bytes 524288 | tf_op jit(solution)/shard_map/all_to_all | solution.py:62
  288.4 117.3 %copy-start.4 = (f32[512]{0:T(512)S(1)}, f32[512]{0:T(512)}, u32[]{:S(2)}) copy-start(f32[512]{0:T(512)} %param.12) | copy-start | bytes 6148
  288.4 128.6 %copy-start.3 = (f32[1,6,16]{2,0,1:T(1,128)S(1)}, f32[1,6,16]{2,0,1:T(1,128)}, u32[]{:S(2)}) copy-start(f32[1,6,16]{2,0,1:T(1,128)} %param.11) | copy-start | bytes 1156
  288.4 128.6 %slice-start = ((f32[512]{0:T(512)}), f32[6]{0:T(128)S(1)}, s32[]{:S(2)}) async-start(f32[512]{0:T(512)} %param.12), calls=%async_computation.7 | async-start | bytes 1024 | tf_op jit(solution)/shard_map/slice | solution.py:80
  390.1 26.7 %all-to-all-start.3 = ((f32[32,1,6,16]{3,1,2,0:T(1,128)}), f32[32,1,6,16]{3,1,2,0:T(1,128)S(1)}, u32[]{:S(2)}, u32[]{:S(2)}) async-start(f32[32,1,6,16]{3,1,2,0:T(1,128)} %copy.44), calls=%async_computation.3 | async-start | bytes 196608 | tf_op jit(solution)/shard_map/all_to_all | solution.py:42
Sparse Core Ops, SparseCore 0:
  11.2 58.7 all-reduce.2
  73.0 133.5 all-reduce.4
Sparse Core Ops, SparseCore 1:
  72.6 215.7 all-gather.1
where the time goes:
time: 427 us; the launch traced here: 426 us
  waiting for transfers between devices  253 us (59%)
  matrix products  87.7 us (21%)
  starting transfers between devices  38.3 us (9%)
  local copies, waits for them, and re-layouts  17.7 us (4%)
  between operations  16.3 us (4%)
  blocking collectives  10.4 us (2%)
    psum x2, waiting for transfers between devices, spread(): array = lax.psum(array, axis)  160 us
    all_gather x1, waiting for transfers between devices, per_device(): lax.all_gather(amp_full, PAIR, axis=0, tiled=True)  81.9 us
    dot_general x16, matrix products, contract(): jnp.einsum('aqd,qbd->ab', halves, factors, preferred_element_type=jnp.flo...  56.9 us
    dot_general x16, matrix products, half_of(): jnp.einsum('qac,cd->aqd', window, amp_pair, preferred_element_type=jnp.fl...  30.7 us
    all_to_all x1, starting transfers between devices, sent_to_all(): lax.all_to_all(jnp.broadcast_to(array[None], (count, *array.shape)), axis...  17.2 us
    all_to_all x1, starting transfers between devices, sent_and_summed(): tiles = lax.all_to_all(cut_along(array, dim, count), axis, 0, 0, tiled=True)  14.9 us
    all_to_all x1, waiting for transfers between devices, sent_and_summed(): tiles = lax.all_to_all(cut_along(array, dim, count), axis, 0, 0, tiled=True)  11.1 us
    all_to_all x1, blocking collectives, per_device(): lax.all_to_all(partial_value, PAIR, split_axis=0, concat_axis=2, tiled=True)  10.4 us
  transfers between devices with their start and end apart: 6, of which 4 were waited for; matrix products, arithmetic and copies ran while one was open for 3% of the time, Pallas kernels for 0%

commit v1 on v0

--- a/solution.py
+++ b/solution.py
@@ -28,7 +28,7 @@
 def spread(array, axes, root):
     array = jnp.where(lax.axis_index(axes) == root, array, jnp.zeros_like(array))
     for axis in axes:
-        array = lax.psum(array, axis)
+        array = jnp.sum(lax.all_gather(array, axis), axis=0)
     return array
 
 

time: 427 us -> 471 us (1.10)
  blocking collectives: 10.4 us -> 42.7 us
  waiting for transfers between devices: 253 us -> 273 us
  starting transfers between devices: 38.3 us -> 30.7 us
  other arithmetic: 2.26 us -> 8.27 us
    psum x2 -> x0, waiting for transfers between devices: 160 us -> none  [spread(): array = lax.psum(array, axis)]
    all_gather x1, waiting for transfers between devices: 81.9 us -> 190 us  [per_device(): lax.all_gather(amp_full, PAIR, axis=0, tiled=True)]
    all_gather x0 -> x2, waiting for transfers between devices: none -> 65.6 us  [spread(): array = jnp.sum(lax.all_gather(array, axis), axis=0)]
    all_to_all x0 -> x1, blocking collectives: none -> 32.3 us  [sent_to_all(): lax.all_to_all(jnp.broadcast_to(array[None], (count, *array.shape)), axis...]
    all_to_all x1 -> x0, starting transfers between devices: 17.2 us -> none  [sent_to_all(): lax.all_to_all(jnp.broadcast_to(array[None], (count, *array.shape)), axis...]
    all_to_all x1, starting transfers between devices: 6.07 us -> 16.1 us  [per_device(): lax.all_to_all(amp_window, PAIR, split_axis=2, concat_axis=0, tiled=True)]
    all_to_all x1, waiting for transfers between devices: 0.01 us -> 6.22 us  [per_device(): lax.all_to_all(amp_window, PAIR, split_axis=2, concat_axis=0, tiled=True)]
    reduce_sum x0 -> x2, other arithmetic: none -> 6 us  [spread(): array = jnp.sum(lax.all_gather(array, axis), axis=0)]
  transfers between devices with their start and end apart: 6 -> 5, of which waited for: 4 -> 5; matrix products, arithmetic and copies ran while one was open for 3% -> 3% of each run, Pallas kernels for 0% -> 0%
where the time goes in v1:
time: 471 us; the launch traced here: 469 us
  waiting for transfers between devices  273 us (58%)
  matrix products  83.7 us (18%)
  blocking collectives  42.7 us (9%)
  starting transfers between devices  30.7 us (7%)
  local copies, waits for them, and re-layouts  16.1 us (3%)
  between operations  14.6 us (3%)
  other arithmetic  8.27 us (2%)
    all_gather x1, waiting for transfers between devices, per_device(): lax.all_gather(amp_full, PAIR, axis=0, tiled=True)  190 us
    all_gather x2, waiting for transfers between devices, spread(): array = jnp.sum(lax.all_gather(array, axis), axis=0)  65.6 us
    dot_general x16, matrix products, contract(): jnp.einsum('aqd,qbd->ab', halves, factors, preferred_element_type=jnp.flo...  56.9 us
    all_to_all x1, blocking collectives, sent_to_all(): lax.all_to_all(jnp.broadcast_to(array[None], (count, *array.shape)), axis...  32.3 us
    dot_general x16, matrix products, half_of(): jnp.einsum('qac,cd->aqd', window, amp_pair, preferred_element_type=jnp.fl...  26.6 us
    all_to_all x1, starting transfers between devices, per_device(): lax.all_to_all(amp_window, PAIR, split_axis=2, concat_axis=0, tiled=True)  16.1 us
    all_to_all x1, starting transfers between devices, sent_and_summed(): tiles = lax.all_to_all(cut_along(array, dim, count), axis, 0, 0, tiled=True)  14.5 us
    all_to_all x1, waiting for transfers between devices, sent_and_summed(): tiles = lax.all_to_all(cut_along(array, dim, count), axis, 0, 0, tiled=True)  11.1 us
  transfers between devices with their start and end apart: 5, of which 5 were waited for; matrix products, arithmetic and copies ran while one was open for 3% of the time, Pallas kernels for 0%

profile of v1, /device:TPU:1, one launch (start us, length us, event | category | flops | bytes accessed | tf_op | source)
XLA Modules:
  0.0 469.3 jit_solution(1987295650036448209)
XLA Ops:
  10.1 50.4 %all-gather.8.cloned.1.call-done = bf16[512,6,512]{2,0,1:T(8,128)(2,1)} async-done(((bf16[128,6,512]{2,0,1:T(8,128)(2,1)}), bf16[512,6,512]{2,0,1:T(8,128)(2,1)}) %all-gather.8.cloned.1.call-update) | async-done | bytes 3145744 | tf_op jit(solution)/shard_map/all_gather | solution.py:31
  64.2 32.3 %all_to_all.43 = bf16[32,1,16,512]{3,2,1,0:T(8,128)(2,1)} all-to-all(bf16[32,1,16,512]{3,2,1,0:T(8,128)(2,1)S(1)} %broadcast_in_dim.25), channel_id=1, replica_groups=mesh['pair_0'=4,'pair_1'=4,'aux'=32] {'aux'}, dimensions={0} | all-to-all | bytes 1048576 | tf_op jit(solution)/shard_map/all_to_all | solution.py:12
  98.1 16.1 %all-to-all-start.1 = ((bf16[1,6,512]{1,0,2:T(2,128)(2,1)}), bf16[1,6,512]{1,0,2:T(2,128)(2,1)S(1)}, u32[]{:S(2)}, u32[]{:S(2)}) async-start(bf16[1,6,512]{1,0,2:T(2,128)(2,1)} %copy.39), calls=%async_computation.1 | async-start | bytes 524288 | tf_op jit(solution)/shard_map/all_to_all | solution.py:62
  114.2 9.2 %copy.38 = bf16[128,32,512]{0,1,2:T(8,128)(2,1)} copy(bf16[128,32,512]{2,1,0:T(8,128)(2,1)} %param.9) | data formatting | bytes 8388608 | tf_op jit(solution)/shard_map/while | solution.py:67
  123.4 6.2 %all-to-all-done.1 = bf16[1,6,512]{1,0,2:T(2,128)(2,1)S(1)} async-done(((bf16[1,6,512]{1,0,2:T(2,128)(2,1)}), bf16[1,6,512]{1,0,2:T(2,128)(2,1)S(1)}, u32[]{:S(2)}, u32[]{:S(2)}) %all-to-all-start.1) | async-done | bytes 6176 | tf_op jit(solution)/shard_map/all_to_all | solution.py:62
  129.8 15.2 %all-gather.10.cloned.1.call-done = bf16[512,6,512]{2,0,1:T(8,128)(2,1)} async-done(((bf16[128,6,512]{2,0,1:T(8,128)(2,1)}), bf16[512,6,512]{2,0,1:T(8,128)(2,1)}) %all-gather.10.cloned.1.call-update) | async-done | bytes 3145744 | tf_op jit(solution)/shard_map/all_gather | solution.py:31
  147.5 189.8 %all-gather.6.cloned.1.call-done = bf16[16,512,512]{2,1,0:T(8,128)(2,1)} async-done(((bf16[1,512,512]{2,1,0:T(8,128)(2,1)}), bf16[16,512,512]{2,1,0:T(8,128)(2,1)}) %all-gather.6.cloned.1.call-update) | async-done | bytes 8388624 | tf_op jit(solution)/shard_map/all_gather | solution.py:67
  337.3 84.9 %while.11 = (s32[]{:T(128)}, f32[16,6,32]{2,0,1:T(8,128)S(1)}, bf16[16,512,512]{2,1,0:T(8,128)(2,1)}, bf16[128,6,512]{2,0,1:T(8,128)(2,1)S(1)}, bf16[128,32,512]{0,1,2:T(8,128)(2,1)}) while((s32[]{:T(128)}, f32[16,6,32]{2,0,1:T(8,128)S(1)}, bf16[16,512,512]{2,1,0:T(8,128)(2,1)}, bf16[128,6,512]{2,0,1:T(8,128)(2,1)S(1)}, ...), condition=%wide.region_3.4_spmd.clone, body=%wide.region_2.3_spmd.sunk.clone | while | flops 428212224 | bytes 7081805 | solution.py:67
  339.0 3.6 convolution_bitcast_fusion.3
  344.3 3.6 convolution_bitcast_fusion.3
  349.6 3.6 convolution_bitcast_fusion.3
  354.9 3.6 convolution_bitcast_fusion.3
  360.2 3.6 convolution_bitcast_fusion.3
  365.5 3.6 convolution_bitcast_fusion.3
  370.8 3.6 convolution_bitcast_fusion.3
  376.1 3.6 convolution_bitcast_fusion.3
  381.4 3.6 convolution_bitcast_fusion.3
  386.7 3.6 convolution_bitcast_fusion.3
  392.0 3.6 convolution_bitcast_fusion.3
  397.3 3.6 convolution_bitcast_fusion.3
  402.7 3.6 convolution_bitcast_fusion.3
  422.5 10.4 %all_to_all.44 = f32[16,1,192]{2,1,0:T(1,128)S(1)} all-to-all(f32[16,1,192]{2,1,0:T(1,128)S(1)} %reshape.73), channel_id=1, replica_groups=mesh['pair_0'=4,'pair_1'=4,'aux'=32] {'pair_0','pair_1'}, dimensions={0} | all-to-all | bytes 24576 | tf_op jit(solution)/shard_map/all_to_all | solution.py:73
  435.0 14.5 %all-to-all-start.3 = ((f32[32,1,6,16]{3,1,2,0:T(1,128)}), f32[32,1,6,16]{3,1,2,0:T(1,128)S(1)}, u32[]{:S(2)}, u32[]{:S(2)}) async-start(f32[32,1,6,16]{3,1,2,0:T(1,128)} %copy.44), calls=%async_computation.3 | async-start | bytes 196608 | tf_op jit(solution)/shard_map/all_to_all | solution.py:42
  450.3 11.1 %all-to-all-done.3 = f32[32,1,6,16]{3,1,2,0:T(1,128)S(1)} async-done(((f32[32,1,6,16]{3,1,2,0:T(1,128)}), f32[32,1,6,16]{3,1,2,0:T(1,128)S(1)}, u32[]{:S(2)}, u32[]{:S(2)}) %all-to-all-start.3) | async-done | bytes 12320 | tf_op jit(solution)/shard_map/all_to_all | solution.py:42
  (91 shorter events, 52.8 us)
Async XLA Ops:
  7.2 415.0 %copy-start = (f32[16,16]{1,0:T(8,128)S(1)}, f32[16,16]{1,0:T(8,128)}, u32[]{:S(2)}) copy-start(f32[16,16]{1,0:T(8,128)} %param.10) | copy-start | bytes 3076
  7.2 53.3 %all-gather.8.cloned.1.call-start = ((), (), s32[]{:S(2)}) async-start(), calls=%async_computation.5 | async-start | bytes 3932160 | tf_op jit(solution)/shard_map/all_gather | solution.py:31
  8.6 55.5 %copy-start.1 = (bf16[1,16,512]{2,1,0:T(8,128)(2,1)S(1)}, bf16[1,16,512]{2,1,0:T(8,128)(2,1)}, u32[]{:S(2)}) copy-start(bf16[1,16,512]{2,1,0:T(8,128)(2,1)} %param.8) | copy-start | bytes 49156
  10.0 135.0 %all-gather.10.cloned.1.call-start = ((), (), s32[]{:S(2)}) async-start(), calls=%async_computation.6 | async-start | bytes 3932160 | tf_op jit(solution)/shard_map/all_gather | solution.py:31
  64.0 273.2 %all-gather.6.cloned.1.call-start = ((), (), s32[]{:S(2)}) async-start(), calls=%async_computation.4 | async-start | bytes 8912896 | tf_op jit(solution)/shard_map/all_gather | solution.py:67
  98.1 31.5 %all-to-all-start.1 = ((bf16[1,6,512]{1,0,2:T(2,128)(2,1)}), bf16[1,6,512]{1,0,2:T(2,128)(2,1)S(1)}, u32[]{:S(2)}, u32[]{:S(2)}) async-start(bf16[1,6,512]{1,0,2:T(2,128)(2,1)} %copy.39), calls=%async_computation.1 | async-start | bytes 524288 | tf_op jit(solution)/shard_map/all_to_all | solution.py:62
  337.3 112.9 %copy-start.3 = (f32[512]{0:T(512)S(1)}, f32[512]{0:T(512)}, u32[]{:S(2)}) copy-start(f32[512]{0:T(512)} %param.12) | copy-start | bytes 6148
  337.3 124.3 %copy-start.2 = (f32[1,6,16]{2,0,1:T(1,128)S(1)}, f32[1,6,16]{2,0,1:T(1,128)}, u32[]{:S(2)}) copy-start(f32[1,6,16]{2,0,1:T(1,128)} %param.11) | copy-start | bytes 1156
  337.3 124.3 %slice-start = ((f32[512]{0:T(512)}), f32[6]{0:T(128)S(1)}, s32[]{:S(2)}) async-start(f32[512]{0:T(512)} %param.12), calls=%async_computation.7 | async-start | bytes 1024 | tf_op jit(solution)/shard_map/slice | solution.py:80
  435.0 26.4 %all-to-all-start.3 = ((f32[32,1,6,16]{3,1,2,0:T(1,128)}), f32[32,1,6,16]{3,1,2,0:T(1,128)S(1)}, u32[]{:S(2)}, u32[]{:S(2)}) async-start(f32[32,1,6,16]{3,1,2,0:T(1,128)} %copy.44), calls=%async_computation.3 | async-start | bytes 196608 | tf_op jit(solution)/shard_map/all_to_all | solution.py:42
Sparse Core Ops, SparseCore 0:
  10.1 50.3 all-gather.7
  64.2 80.8 all-gather.9
  147.1 190.1 all-gather.5
